TPU v7x, 32 devices: a whole 2x2x4 slice. The times are simulated.
32 devices in a mesh: leaf: 8 (over z, x), sub: 4 (over y, core).
Axes of the slice: x: 2, y: 2, z: 4, core: 2. Of those that a mesh axis runs over, the one named last changes fastest.
Arguments:
- points: bfloat16 [96, 64, 512], P('leaf', None, 'sub'), may hold values from -5 to 5
- charges: bfloat16 [96, 8, 512], P('leaf', None, 'sub'), may hold values from -6 to 6
- near_leaf: int32 [96, 32], P('leaf'), may hold values from -1 to 95, as said below
- far_node: int32 [96, 32], P('leaf'), may hold values from 0 to 31
- skel_index: int32 [32, 256], P(('leaf', 'sub')), may hold values from 0 to 1535, as said below
- skel_weight: bfloat16 [32, 8, 256], P(('leaf', 'sub')), may hold values from -12 to 12
Outputs:
- potential: float32 [96, 8, 512], P('leaf', None, 'sub')
Inputs may be any that keep to these rules, and one draw needn't show every extreme that they name: `near_leaf`: entry 0 of the list of leaf l is l itself; every other entry is -1 or a leaf held by another index of leaf. Over the lists of the 12 leaves of one index of leaf no leaf appears twice, and at most 3 distinct leaves of any one other index of leaf appear (leaves k * 12 to k * 12 + 11 belong to index k); every draw reaches 3. `skel_index`: the 256 entries of a row are distinct.
All inputs are finite; a program needn't handle non-finite values.
Results may differ from a plain program's by a relative error of at most 0.0003.
Values may be sent and summed in bfloat16 or wider, within the bound.
A program may use at most 64 MiB of HBM per device.

v0:
```python
import jax
import jax.numpy as jnp
from jax import lax
from jax.sharding import PartitionSpec as P

CAP = 3
RATE_SCALE = 2.5


def kernel_apply(targets, sources, weights):
    target_wide = targets.astype(jnp.float32)
    target_sq = jnp.sum(target_wide * target_wide, axis=0)
    source_sq = jnp.sum(jnp.square(sources.astype(jnp.float32)), axis=1)
    inner_prod = jnp.einsum("dr,mdc->rmc", targets, sources, preferred_element_type=jnp.float32)
    distance = target_sq[:, None, None] + source_sq[None] - 2.0 * inner_prod
    decay_rate = RATE_SCALE / targets.shape[0]
    kernel_block = jnp.exp(-decay_rate * distance)
    return jnp.einsum(
        "rmc,mkc->kr", kernel_block, weights.astype(jnp.float32), precision=lax.Precision.HIGHEST
    )


def shards(points, charges, near_leaf, far_node, skel_index, skel_weight):
    leaf_dev, features, quarter = points.shape
    leaf_count = lax.axis_size("leaf")
    own_index = lax.axis_index("leaf")
    slot_count = CAP
    leaves_all = leaf_count * leaf_dev
    entries = near_leaf.reshape(-1)
    live_flat = entries >= 0
    all_ids = jnp.arange(leaves_all, dtype=jnp.int32)
    lane_ids = jnp.arange(leaf_count, dtype=jnp.int32)
    other_row = lane_ids != own_index
    matches = entries[:, None] == all_ids[None, :]
    wanted = jnp.any(matches, axis=0).reshape(leaf_count, leaf_dev) & other_row[:, None]
    wanted_int = wanted.astype(jnp.int32)
    slot_rank = jnp.cumsum(wanted_int, axis=1) - 1
    asked_mask = lax.all_to_all(wanted_int, "leaf", split_axis=0, concat_axis=0, tiled=True)
    asked_rank = jnp.cumsum(asked_mask, axis=1) - 1
    slot_ids = jnp.arange(slot_count, dtype=jnp.int32)
    selector = (
        (asked_mask[:, None, :] == 1) & (asked_rank[:, None, :] == slot_ids[None, :, None])
    ).astype(jnp.bfloat16)
    send_points = jnp.einsum(
        "dcj,jkq->dckq", selector, points, preferred_element_type=jnp.float32
    ).astype(jnp.bfloat16)
    send_charges = jnp.einsum(
        "dcj,jkq->dckq", selector, charges, preferred_element_type=jnp.float32
    ).astype(jnp.bfloat16)
    got_points, got_charges = (
        lax.all_to_all(send_points, "leaf", split_axis=0, concat_axis=0, tiled=True),
        lax.all_to_all(send_charges, "leaf", split_axis=0, concat_axis=0, tiled=True),
    )
    table_points = jnp.concatenate(
        [points, got_points.reshape(leaf_count * slot_count, features, quarter)], axis=0
    )
    table_charges = jnp.concatenate(
        [charges, got_charges.reshape(leaf_count * slot_count, charges.shape[1], quarter)], axis=0
    )
    slot_pos = leaf_dev + lane_ids[:, None] * slot_count + slot_rank
    local_pos = jnp.broadcast_to(
        jnp.arange(leaf_dev, dtype=jnp.int32)[None, :], (leaf_count, leaf_dev)
    )
    pos_table = jnp.where(other_row[:, None], slot_pos, local_pos).reshape(-1)
    position = jnp.sum(jnp.where(matches, pos_table[None, :], 0), axis=1)
    position = position.reshape(leaf_dev, -1)
    live_mask = live_flat.reshape(leaf_dev, -1)
    whole_targets = lax.all_gather(points, "sub", axis=2, tiled=True)

    def near_targets(pieces):
        target, where_from, alive = pieces
        weights = jnp.where(
            alive[:, None, None], table_charges[where_from], jnp.zeros((), jnp.bfloat16)
        )
        return kernel_apply(target, table_points[where_from], weights)

    partial_value = lax.map(near_targets, (whole_targets, position, live_mask))
    near_term = lax.psum_scatter(partial_value, "sub", scatter_dimension=2, tiled=True)
    node_dev, skel_size = skel_index.shape
    flat_points = jnp.transpose(points, (1, 0, 2)).reshape(features, leaf_dev * quarter)
    picked = jnp.take(flat_points, skel_index.reshape(-1), axis=1)
    skel_points = jnp.transpose(picked.reshape(features, node_dev, skel_size), (1, 0, 2))
    all_skel, all_weight = (
        lax.all_gather(skel_points, ("leaf", "sub"), axis=0, tiled=True),
        lax.all_gather(skel_weight, ("leaf", "sub"), axis=0, tiled=True),
    )

    def far_sum(pieces):
        target, node_list = pieces
        return kernel_apply(target, all_skel[node_list], all_weight[node_list])

    far_term = lax.map(far_sum, (points, far_node))
    return near_term + far_term


def solution(mesh):
    in_specs = (
        P("leaf", None, "sub"),
        P("leaf", None, "sub"),
        P("leaf", None),
        P("leaf", None),
        P(("leaf", "sub"), None),
        P(("leaf", "sub"), None, None),
    )
    out_specs = P("leaf", None, "sub")
    return jax.shard_map(shards, mesh=mesh, in_specs=in_specs, out_specs=out_specs, check_vma=False)
```

profile of v0, /device:TPU:0, one launch (start us, length us, event | category | flops | bytes accessed | tf_op | source)
XLA Modules:
  0.0 407.2 jit_solution(3622828070690735007)
XLA Ops:
  9.1 7.3 %all-to-all-start = ((s32[8,1,12]{2,1,0:T(1,128)}), s32[8,1,12]{2,1,0:T(1,128)S(1)}, u32[]{:S(2)}, u32[]{:S(2)}) async-start(s32[8,1,12]{2,1,0:T(1,128)} %bitcast.13), calls=%async_computation | async-start | bytes 8192 | tf_op jit(solution)/shard_map/all_to_all | solution.py:38
  39.2 42.6 %all_gather.10 = bf16[32,8,256]{2,1,0:T(8,128)(2,1)S(1)} all-gather(bf16[1,8,256]{2,1,0:T(8,128)(2,1)} %param.15), channel_id=1, replica_groups=mesh['leaf'=8,'sub'=4] {'leaf','sub'}, dimensions={0}, use_global_device_ids=true | all-gather | bytes 135168 | tf_op jit(solution)/shard_map/all_gather | solution.py:85
  82.5 8.9 %all_gather.9 = bf16[12,64,512]{2,1,0:T(8,128)(2,1)S(1)} all-gather(bf16[12,64,128]{2,1,0:T(8,128)(2,1)} %param.10), channel_id=1, replica_groups=mesh['leaf'=8,'sub'=4] {'sub'}, dimensions={2}, use_global_device_ids=true | all-gather | bytes 983040 | tf_op jit(solution)/shard_map/all_gather | solution.py:68
  91.5 173.4 %while.20 = (s32[]{:T(128)}, f32[12,8,512]{2,1,0:T(8,128)}, pred[12,32]{1,0:T(8,128)(4,1)S(1)}, s32[12,32]{1,0:T(8,128)S(1)}, bf16[36,8,128]{2,1,0:T(8,128)(2,1)...) while((s32[]{:T(128)}, f32[12,8,512]{2,1,0:T(8,128)}, ...), condition=%wide.region_7.8_spmd, body=%wide.region_4.7_spmd.sunk | while | flops 479064672 | bytes 19260740 | solution.py:77
  97.5 8.5 %fusion.88 = f32[12,8,512]{2,1,0:T(8,128)} fusion(f32[12,8,512]{2,1,0:T(8,128)} %get-tuple-element.203, s32[]{:T(128)} %get-tuple-element.202, f32[512,32,128]{2,0,1:T(8,128)} %fusion.87, f32[32,128]{1,0:T(8,128)S(1)} %multiply_reduce_fusion.8, f32[512]{0:T(512)S(1)} %multiply_reduce_fusion.9, bf16[32,8,128]{2,1,0:T(8,128)(2,1)S(1)} %gather_fusion.1, ...), kind=kOutput, calls=%fused_computation.16.clone.1 | convolution fusion | flops 209747968 | bytes 8489504 | tf_op jit(solution)/shard_map/while/body/eval_jaxpr/rmc,mkc->kr/dot_general | solution.py:18
  112.0 8.5 %fusion.88 = f32[12,8,512]{2,1,0:T(8,128)} fusion(f32[12,8,512]{2,1,0:T(8,128)} %get-tuple-element.203, s32[]{:T(128)} %get-tuple-element.202, f32[512,32,128]{2,0,1:T(8,128)} %fusion.87, f32[32,128]{1,0:T(8,128)S(1)} %multiply_reduce_fusion.8, f32[512]{0:T(512)S(1)} %multiply_reduce_fusion.9, bf16[32,8,128]{2,1,0:T(8,128)(2,1)S(1)} %gather_fusion.1, ...), kind=kOutput, calls=%fused_computation.16.clone.1 | convolution fusion | flops 209747968 | bytes 8489504 | tf_op jit(solution)/shard_map/while/body/eval_jaxpr/rmc,mkc->kr/dot_general | solution.py:18
  126.4 8.5 %fusion.88 = f32[12,8,512]{2,1,0:T(8,128)} fusion(f32[12,8,512]{2,1,0:T(8,128)} %get-tuple-element.203, s32[]{:T(128)} %get-tuple-element.202, f32[512,32,128]{2,0,1:T(8,128)} %fusion.87, f32[32,128]{1,0:T(8,128)S(1)} %multiply_reduce_fusion.8, f32[512]{0:T(512)S(1)} %multiply_reduce_fusion.9, bf16[32,8,128]{2,1,0:T(8,128)(2,1)S(1)} %gather_fusion.1, ...), kind=kOutput, calls=%fused_computation.16.clone.1 | convolution fusion | flops 209747968 | bytes 8489504 | tf_op jit(solution)/shard_map/while/body/eval_jaxpr/rmc,mkc->kr/dot_general | solution.py:18
  140.9 8.5 %fusion.88 = f32[12,8,512]{2,1,0:T(8,128)} fusion(f32[12,8,512]{2,1,0:T(8,128)} %get-tuple-element.203, s32[]{:T(128)} %get-tuple-element.202, f32[512,32,128]{2,0,1:T(8,128)} %fusion.87, f32[32,128]{1,0:T(8,128)S(1)} %multiply_reduce_fusion.8, f32[512]{0:T(512)S(1)} %multiply_reduce_fusion.9, bf16[32,8,128]{2,1,0:T(8,128)(2,1)S(1)} %gather_fusion.1, ...), kind=kOutput, calls=%fused_computation.16.clone.1 | convolution fusion | flops 209747968 | bytes 8489504 | tf_op jit(solution)/shard_map/while/body/eval_jaxpr/rmc,mkc->kr/dot_general | solution.py:18
  155.3 8.5 %fusion.88 = f32[12,8,512]{2,1,0:T(8,128)} fusion(f32[12,8,512]{2,1,0:T(8,128)} %get-tuple-element.203, s32[]{:T(128)} %get-tuple-element.202, f32[512,32,128]{2,0,1:T(8,128)} %fusion.87, f32[32,128]{1,0:T(8,128)S(1)} %multiply_reduce_fusion.8, f32[512]{0:T(512)S(1)} %multiply_reduce_fusion.9, bf16[32,8,128]{2,1,0:T(8,128)(2,1)S(1)} %gather_fusion.1, ...), kind=kOutput, calls=%fused_computation.16.clone.1 | convolution fusion | flops 209747968 | bytes 8489504 | tf_op jit(solution)/shard_map/while/body/eval_jaxpr/rmc,mkc->kr/dot_general | solution.py:18
  169.8 8.5 %fusion.88 = f32[12,8,512]{2,1,0:T(8,128)} fusion(f32[12,8,512]{2,1,0:T(8,128)} %get-tuple-element.203, s32[]{:T(128)} %get-tuple-element.202, f32[512,32,128]{2,0,1:T(8,128)} %fusion.87, f32[32,128]{1,0:T(8,128)S(1)} %multiply_reduce_fusion.8, f32[512]{0:T(512)S(1)} %multiply_reduce_fusion.9, bf16[32,8,128]{2,1,0:T(8,128)(2,1)S(1)} %gather_fusion.1, ...), kind=kOutput, calls=%fused_computation.16.clone.1 | convolution fusion | flops 209747968 | bytes 8489504 | tf_op jit(solution)/shard_map/while/body/eval_jaxpr/rmc,mkc->kr/dot_general | solution.py:18
  184.2 8.5 %fusion.88 = f32[12,8,512]{2,1,0:T(8,128)} fusion(f32[12,8,512]{2,1,0:T(8,128)} %get-tuple-element.203, s32[]{:T(128)} %get-tuple-element.202, f32[512,32,128]{2,0,1:T(8,128)} %fusion.87, f32[32,128]{1,0:T(8,128)S(1)} %multiply_reduce_fusion.8, f32[512]{0:T(512)S(1)} %multiply_reduce_fusion.9, bf16[32,8,128]{2,1,0:T(8,128)(2,1)S(1)} %gather_fusion.1, ...), kind=kOutput, calls=%fused_computation.16.clone.1 | convolution fusion | flops 209747968 | bytes 8489504 | tf_op jit(solution)/shard_map/while/body/eval_jaxpr/rmc,mkc->kr/dot_general | solution.py:18
  198.7 8.5 %fusion.88 = f32[12,8,512]{2,1,0:T(8,128)} fusion(f32[12,8,512]{2,1,0:T(8,128)} %get-tuple-element.203, s32[]{:T(128)} %get-tuple-element.202, f32[512,32,128]{2,0,1:T(8,128)} %fusion.87, f32[32,128]{1,0:T(8,128)S(1)} %multiply_reduce_fusion.8, f32[512]{0:T(512)S(1)} %multiply_reduce_fusion.9, bf16[32,8,128]{2,1,0:T(8,128)(2,1)S(1)} %gather_fusion.1, ...), kind=kOutput, calls=%fused_computation.16.clone.1 | convolution fusion | flops 209747968 | bytes 8489504 | tf_op jit(solution)/shard_map/while/body/eval_jaxpr/rmc,mkc->kr/dot_general | solution.py:18
  213.1 8.5 %fusion.88 = f32[12,8,512]{2,1,0:T(8,128)} fusion(f32[12,8,512]{2,1,0:T(8,128)} %get-tuple-element.203, s32[]{:T(128)} %get-tuple-element.202, f32[512,32,128]{2,0,1:T(8,128)} %fusion.87, f32[32,128]{1,0:T(8,128)S(1)} %multiply_reduce_fusion.8, f32[512]{0:T(512)S(1)} %multiply_reduce_fusion.9, bf16[32,8,128]{2,1,0:T(8,128)(2,1)S(1)} %gather_fusion.1, ...), kind=kOutput, calls=%fused_computation.16.clone.1 | convolution fusion | flops 209747968 | bytes 8489504 | tf_op jit(solution)/shard_map/while/body/eval_jaxpr/rmc,mkc->kr/dot_general | solution.py:18
  227.6 8.5 %fusion.88 = f32[12,8,512]{2,1,0:T(8,128)} fusion(f32[12,8,512]{2,1,0:T(8,128)} %get-tuple-element.203, s32[]{:T(128)} %get-tuple-element.202, f32[512,32,128]{2,0,1:T(8,128)} %fusion.87, f32[32,128]{1,0:T(8,128)S(1)} %multiply_reduce_fusion.8, f32[512]{0:T(512)S(1)} %multiply_reduce_fusion.9, bf16[32,8,128]{2,1,0:T(8,128)(2,1)S(1)} %gather_fusion.1, ...), kind=kOutput, calls=%fused_computation.16.clone.1 | convolution fusion | flops 209747968 | bytes 8489504 | tf_op jit(solution)/shard_map/while/body/eval_jaxpr/rmc,mkc->kr/dot_general | solution.py:18
  242.0 8.5 %fusion.88 = f32[12,8,512]{2,1,0:T(8,128)} fusion(f32[12,8,512]{2,1,0:T(8,128)} %get-tuple-element.203, s32[]{:T(128)} %get-tuple-element.202, f32[512,32,128]{2,0,1:T(8,128)} %fusion.87, f32[32,128]{1,0:T(8,128)S(1)} %multiply_reduce_fusion.8, f32[512]{0:T(512)S(1)} %multiply_reduce_fusion.9, bf16[32,8,128]{2,1,0:T(8,128)(2,1)S(1)} %gather_fusion.1, ...), kind=kOutput, calls=%fused_computation.16.clone.1 | convolution fusion | flops 209747968 | bytes 8489504 | tf_op jit(solution)/shard_map/while/body/eval_jaxpr/rmc,mkc->kr/dot_general | solution.py:18
  256.5 8.5 %fusion.88 = f32[12,8,512]{2,1,0:T(8,128)} fusion(f32[12,8,512]{2,1,0:T(8,128)} %get-tuple-element.203, s32[]{:T(128)} %get-tuple-element.202, f32[512,32,128]{2,0,1:T(8,128)} %fusion.87, f32[32,128]{1,0:T(8,128)S(1)} %multiply_reduce_fusion.8, f32[512]{0:T(512)S(1)} %multiply_reduce_fusion.9, bf16[32,8,128]{2,1,0:T(8,128)(2,1)S(1)} %gather_fusion.1, ...), kind=kOutput, calls=%fused_computation.16.clone.1 | convolution fusion | flops 209747968 | bytes 8489504 | tf_op jit(solution)/shard_map/while/body/eval_jaxpr/rmc,mkc->kr/dot_general | solution.py:18
  265.0 133.3 %while.21 = (s32[]{:T(128)}, f32[12,8,128]{2,1,0:T(8,128)S(1)}, s32[12,32]{1,0:T(8,128)}, bf16[32,8,256]{2,1,0:T(8,128)(2,1)S(1)}, bf16[12,64,128]{2,1,0:T(8,128...) while((s32[]{:T(128)}, f32[12,8,128]{2,1,0:T(8,128)S(1)}, s32[12,32]{1,0:T(8,128)}, ...), condition=%wide.region_12.13_spmd, body=%wide.region_9.12_spmd.sunk | while | flops 240665568 | bytes 13084381 | solution.py:92
  282.3 5.0 %fusion.95 = f32[12,8,128]{2,1,0:T(8,128)S(1)} fusion(f32[12,8,128]{2,1,0:T(8,128)S(1)} %get-tuple-element.226, s32[]{:T(128)} %get-tuple-element.225, bf16[32,8,256]{2,1,0:T(8,128)(2,1)S(1)} %gather_fusion.2, f32[128,32,256]{2,0,1:T(8,128)} %fusion.94, f32[32,256]{1,0:T(8,128)S(1)} %multiply_reduce_fusion.10, f32[128]{0:T(128)S(1)} %multiply_reduce_fusion.11), kind=kOutput, calls=%fused_computation.47.clone.1 | convolution fusion | flops 104857600 | bytes 4362756 | tf_op jit(solution)/shard_map/while/body/eval_jaxpr/rmc,mkc->kr/dot_general | solution.py:18
  293.4 5.0 %fusion.95 = f32[12,8,128]{2,1,0:T(8,128)S(1)} fusion(f32[12,8,128]{2,1,0:T(8,128)S(1)} %get-tuple-element.226, s32[]{:T(128)} %get-tuple-element.225, bf16[32,8,256]{2,1,0:T(8,128)(2,1)S(1)} %gather_fusion.2, f32[128,32,256]{2,0,1:T(8,128)} %fusion.94, f32[32,256]{1,0:T(8,128)S(1)} %multiply_reduce_fusion.10, f32[128]{0:T(128)S(1)} %multiply_reduce_fusion.11), kind=kOutput, calls=%fused_computation.47.clone.1 | convolution fusion | flops 104857600 | bytes 4362756 | tf_op jit(solution)/shard_map/while/body/eval_jaxpr/rmc,mkc->kr/dot_general | solution.py:18
  304.5 5.0 %fusion.95 = f32[12,8,128]{2,1,0:T(8,128)S(1)} fusion(f32[12,8,128]{2,1,0:T(8,128)S(1)} %get-tuple-element.226, s32[]{:T(128)} %get-tuple-element.225, bf16[32,8,256]{2,1,0:T(8,128)(2,1)S(1)} %gather_fusion.2, f32[128,32,256]{2,0,1:T(8,128)} %fusion.94, f32[32,256]{1,0:T(8,128)S(1)} %multiply_reduce_fusion.10, f32[128]{0:T(128)S(1)} %multiply_reduce_fusion.11), kind=kOutput, calls=%fused_computation.47.clone.1 | convolution fusion | flops 104857600 | bytes 4362756 | tf_op jit(solution)/shard_map/while/body/eval_jaxpr/rmc,mkc->kr/dot_general | solution.py:18
  315.6 5.0 %fusion.95 = f32[12,8,128]{2,1,0:T(8,128)S(1)} fusion(f32[12,8,128]{2,1,0:T(8,128)S(1)} %get-tuple-element.226, s32[]{:T(128)} %get-tuple-element.225, bf16[32,8,256]{2,1,0:T(8,128)(2,1)S(1)} %gather_fusion.2, f32[128,32,256]{2,0,1:T(8,128)} %fusion.94, f32[32,256]{1,0:T(8,128)S(1)} %multiply_reduce_fusion.10, f32[128]{0:T(128)S(1)} %multiply_reduce_fusion.11), kind=kOutput, calls=%fused_computation.47.clone.1 | convolution fusion | flops 104857600 | bytes 4362756 | tf_op jit(solution)/shard_map/while/body/eval_jaxpr/rmc,mkc->kr/dot_general | solution.py:18
  360.0 5.0 %fusion.95 = f32[12,8,128]{2,1,0:T(8,128)S(1)} fusion(f32[12,8,128]{2,1,0:T(8,128)S(1)} %get-tuple-element.226, s32[]{:T(128)} %get-tuple-element.225, bf16[32,8,256]{2,1,0:T(8,128)(2,1)S(1)} %gather_fusion.2, f32[128,32,256]{2,0,1:T(8,128)} %fusion.94, f32[32,256]{1,0:T(8,128)S(1)} %multiply_reduce_fusion.10, f32[128]{0:T(128)S(1)} %multiply_reduce_fusion.11), kind=kOutput, calls=%fused_computation.47.clone.1 | convolution fusion | flops 104857600 | bytes 4362756 | tf_op jit(solution)/shard_map/while/body/eval_jaxpr/rmc,mkc->kr/dot_general | solution.py:18
  371.1 5.0 %fusion.95 = f32[12,8,128]{2,1,0:T(8,128)S(1)} fusion(f32[12,8,128]{2,1,0:T(8,128)S(1)} %get-tuple-element.226, s32[]{:T(128)} %get-tuple-element.225, bf16[32,8,256]{2,1,0:T(8,128)(2,1)S(1)} %gather_fusion.2, f32[128,32,256]{2,0,1:T(8,128)} %fusion.94, f32[32,256]{1,0:T(8,128)S(1)} %multiply_reduce_fusion.10, f32[128]{0:T(128)S(1)} %multiply_reduce_fusion.11), kind=kOutput, calls=%fused_computation.47.clone.1 | convolution fusion | flops 104857600 | bytes 4362756 | tf_op jit(solution)/shard_map/while/body/eval_jaxpr/rmc,mkc->kr/dot_general | solution.py:18
  382.2 5.0 %fusion.95 = f32[12,8,128]{2,1,0:T(8,128)S(1)} fusion(f32[12,8,128]{2,1,0:T(8,128)S(1)} %get-tuple-element.226, s32[]{:T(128)} %get-tuple-element.225, bf16[32,8,256]{2,1,0:T(8,128)(2,1)S(1)} %gather_fusion.2, f32[128,32,256]{2,0,1:T(8,128)} %fusion.94, f32[32,256]{1,0:T(8,128)S(1)} %multiply_reduce_fusion.10, f32[128]{0:T(128)S(1)} %multiply_reduce_fusion.11), kind=kOutput, calls=%fused_computation.47.clone.1 | convolution fusion | flops 104857600 | bytes 4362756 | tf_op jit(solution)/shard_map/while/body/eval_jaxpr/rmc,mkc->kr/dot_general | solution.py:18
  (233 shorter events, 196.1 us)
Async XLA Ops:
  7.4 84.1 %copy-start = (bf16[12,64,128]{2,1,0:T(8,128)(2,1)S(1)}, bf16[12,64,128]{2,1,0:T(8,128)(2,1)}, u32[]{:S(2)}) copy-start(bf16[12,64,128]{2,1,0:T(8,128)(2,1)} %param.10) | copy-start | bytes 589828
  7.4 84.1 %copy-start.1 = (bf16[12,8,128]{2,1,0:T(8,128)(2,1)S(1)}, bf16[12,8,128]{2,1,0:T(8,128)(2,1)}, u32[]{:S(2)}) copy-start(bf16[12,8,128]{2,1,0:T(8,128)(2,1)} %param.11) | copy-start | bytes 73732
  9.1 13.6 %all-to-all-start = ((s32[8,1,12]{2,1,0:T(1,128)}), s32[8,1,12]{2,1,0:T(1,128)S(1)}, u32[]{:S(2)}, u32[]{:S(2)}) async-start(s32[8,1,12]{2,1,0:T(1,128)} %bitcast.13), calls=%async_computation | async-start | bytes 8192 | tf_op jit(solution)/shard_map/all_to_all | solution.py:38
  16.3 248.7 %all-gather.2.cloned.1.call-start = ((), (), s32[]{:S(2)}) async-start(), calls=%async_computation.5 | async-start | bytes 1081344 | tf_op jit(solution)/shard_map/all_gather | solution.py:84
  24.4 11.3 %all-to-all-start.1 = ((bf16[8,3,8,128]{3,2,1,0:T(8,128)(2,1)}), bf16[8,3,8,128]{3,2,1,0:T(8,128)(2,1)S(1)}, u32[]{:S(2)}, u32[]{:S(2)}) async-start(bf16[8,3,8,128]{3,2,1,0:T(8,128)(2,1)} %copy.28), calls=%async_computation.1 | async-start | bytes 98304 | tf_op jit(solution)/shard_map/all_to_all | solution.py:52
  35.7 55.7 %all-to-all-start.2 = ((bf16[8,3,64,128]{3,2,1,0:T(8,128)(2,1)}), bf16[8,3,64,128]{3,2,1,0:T(8,128)(2,1)S(1)}, u32[]{:S(2)}, u32[]{:S(2)}) async-start(bf16[8,3,64,128]{3,2,1,0:T(8,128)(2,1)} %copy.30), calls=%async_computation.2 | async-start | bytes 786432 | tf_op jit(solution)/shard_map/all_to_all | solution.py:51
  39.2 359.1 %reduce-scatter.2.cloned.1.call-start = ((), (), s32[]{:S(2)}) async-start(), calls=%async_computation.4 | async-start | bytes 245760 | tf_op jit(solution)/shard_map/reduce_scatter | solution.py:78
Sparse Core Ops, SparseCore 0:
  20.7 56.8 all-gather.1
Sparse Core Ops, SparseCore 1:
  265.1 15.8 reduce-scatter.1
where the time goes:
time: 409 us; the launch traced here: 407 us
  matrix products  250 us (61%)
  blocking collectives  51.5 us (13%)
  local copies, waits for them, and re-layouts  49.3 us (12%)
  other arithmetic  19.5 us (5%)
  starting transfers between devices  15.3 us (4%)
  between operations  15 us (4%)
  waiting for transfers between devices  6.28 us (2%)
    dot_general x24, matrix products, kernel_apply(): jnp.einsum('rmc,mkc->kr', kernel_block, weights.astype(jnp.float32), prec...  162 us
    dot_general x24, matrix products, kernel_apply(): jnp.einsum('dr,mdc->rmc', targets, sources, preferred_element_type=jnp.fl...  86 us
    all_gather x1, blocking collectives, shards(): lax.all_gather(skel_weight, ('leaf', 'sub'), axis=0, tiled=True)  42.6 us
    gather x24, local copies, waits for them, and re-layouts, far_sum(): return kernel_apply(target, all_skel[node_list], all_weight[node_list])  28.9 us
    all_gather x1, blocking collectives, shards(): whole_targets = lax.all_gather(points, 'sub', axis=2, tiled=True)  8.93 us
    select_n x12, other arithmetic, far_sum(): return kernel_apply(target, all_skel[node_list], all_weight[node_list])  8.59 us
  transfers between devices with their start and end apart: 5, of which 2 were waited for; matrix products, arithmetic and copies ran while one was open for 77% of the time, Pallas kernels for 0%

commit v1 on v0

--- a/solution.py
+++ b/solution.py
@@ -5,6 +5,28 @@
 
 CAP = 3
 RATE_SCALE = 2.5
+
+
+def laid_out(pieces, dim):
+    pieces = jnp.moveaxis(pieces, 0, dim)
+    lengths = pieces.shape
+    return pieces.reshape(*lengths[:dim], lengths[dim] * lengths[dim + 1], *lengths[dim + 2 :])
+
+
+def collected_by_bits(shard, axis):
+    size = lax.axis_size(axis)
+    blocks = shard[None]
+    for level in range(size.bit_length() - 1):
+        bit = 1 << level
+        other = lax.ppermute(blocks, axis, [(i, i ^ bit) for i in range(size)])
+        both = jnp.stack([blocks, other])
+        upper = lax.axis_index(axis) >> level & 1
+        blocks = jnp.where(upper == 0, both, both[::-1]).reshape(-1, *shard.shape)
+    return blocks
+
+
+def gather_by_bits(shard, axis, dim):
+    return laid_out(collected_by_bits(shard, axis), dim)
 
 
 def kernel_apply(targets, sources, weights):
@@ -82,7 +104,7 @@
     skel_points = jnp.transpose(picked.reshape(features, node_dev, skel_size), (1, 0, 2))
     all_skel, all_weight = (
         lax.all_gather(skel_points, ("leaf", "sub"), axis=0, tiled=True),
-        lax.all_gather(skel_weight, ("leaf", "sub"), axis=0, tiled=True),
+        gather_by_bits(skel_weight, ("leaf", "sub"), 0),
     )
 
     def far_sum(pieces):

time: 409 us -> 335 us (0.82)
  matrix products: 250 us -> 201 us
  blocking collectives: 51.5 us -> 9.06 us
  starting transfers between devices: 15.3 us -> 23.8 us
  waiting for transfers between devices: 6.28 us -> 14.7 us
    all_gather x1 -> x0, blocking collectives: 42.6 us -> none  [shards(): lax.all_gather(skel_weight, ('leaf', 'sub'), axis=0, tiled=True)]
    dot_general x24, matrix products: 162 us -> 136 us  [kernel_apply(): jnp.einsum('rmc,mkc->kr', kernel_block, weights.astype(jnp.float32), prec...]
    dot_general x24, matrix products: 86 us -> 62.8 us  [kernel_apply(): jnp.einsum('dr,mdc->rmc', targets, sources, preferred_element_type=jnp.fl...]
    ppermute x0 -> x5, waiting for transfers between devices: none -> 12 us  [collected_by_bits(): other = lax.ppermute(blocks, axis, [(i, i ^ bit) for i in range(size)])]
    ppermute x0 -> x5, starting transfers between devices: none -> 8.5 us  [collected_by_bits(): other = lax.ppermute(blocks, axis, [(i, i ^ bit) for i in range(size)])]
  transfers between devices with their start and end apart: 5 -> 10, of which waited for: 2 -> 3; matrix products, arithmetic and copies ran while one was open for 77% -> 80% of each run, Pallas kernels for 0% -> 0%
where the time goes in v1:
time: 335 us; the launch traced here: 333 us
  matrix products  201 us (60%)
  local copies, waits for them, and re-layouts  49.2 us (15%)
  starting transfers between devices  23.8 us (7%)
  other arithmetic  20.3 us (6%)
  between operations  15 us (4%)
  waiting for transfers between devices  14.7 us (4%)
  blocking collectives  9.06 us (3%)
    dot_general x24, matrix products, kernel_apply(): jnp.einsum('rmc,mkc->kr', kernel_block, weights.astype(jnp.float32), prec...  136 us
    dot_general x24, matrix products, kernel_apply(): jnp.einsum('dr,mdc->rmc', targets, sources, preferred_element_type=jnp.fl...  62.8 us
    gather x24, local copies, waits for them, and re-layouts, far_sum(): return kernel_apply(target, all_skel[node_list], all_weight[node_list])  28.9 us
    ppermute x5, waiting for transfers between devices, collected_by_bits(): other = lax.ppermute(blocks, axis, [(i, i ^ bit) for i in range(size)])  12 us
    all_gather x1, blocking collectives, shards(): whole_targets = lax.all_gather(points, 'sub', axis=2, tiled=True)  9.06 us
    select_n x12, other arithmetic, far_sum(): return kernel_apply(target, all_skel[node_list], all_weight[node_list])  8.58 us
    ppermute x5, starting transfers between devices, collected_by_bits(): other = lax.ppermute(blocks, axis, [(i, i ^ bit) for i in range(size)])  8.5 us
    gather x12, local copies, waits for them, and re-layouts, near_targets(): return kernel_apply(target, table_points[where_from], weights)  7.76 us
  transfers between devices with their start and end apart: 10, of which 3 were waited for; matrix products, arithmetic and copies ran while one was open for 80% of the time, Pallas kernels for 0%

profile of v1, /device:TPU:0, one launch (start us, length us, event | category | flops | bytes accessed | tf_op | source)
XLA Modules:
  0.0 333.3 jit_solution(15807581544696674657)
XLA Ops:
  9.1 7.3 %all-to-all-start = ((s32[8,1,12]{2,1,0:T(1,128)}), s32[8,1,12]{2,1,0:T(1,128)S(1)}, u32[]{:S(2)}, u32[]{:S(2)}) async-start(s32[8,1,12]{2,1,0:T(1,128)} %bitcast.13), calls=%async_computation | async-start | bytes 8192 | tf_op jit(solution)/shard_map/all_to_all | solution.py:60
  21.5 9.1 %all_gather.6 = bf16[12,64,512]{2,1,0:T(8,128)(2,1)S(1)} all-gather(bf16[12,64,128]{2,1,0:T(8,128)(2,1)} %param.10), channel_id=1, replica_groups=mesh['leaf'=8,'sub'=4] {'sub'}, dimensions={2}, use_global_device_ids=true | all-gather | bytes 983040 | tf_op jit(solution)/shard_map/all_gather | solution.py:90
  39.2 4.5 %all-to-all-start.1 = ((bf16[8,3,8,128]{3,2,1,0:T(8,128)(2,1)}), bf16[8,3,8,128]{3,2,1,0:T(8,128)(2,1)S(1)}, u32[]{:S(2)}, u32[]{:S(2)}) async-start(bf16[8,3,8,128]{3,2,1,0:T(8,128)(2,1)} %copy.31), calls=%async_computation.1 | async-start | bytes 98304 | tf_op jit(solution)/shard_map/all_to_all | solution.py:74
  56.9 9.8 %collective-permute-done.4 = bf16[16,1,8,256]{3,2,0,1:T(8,128)(2,1)S(1)} collective-permute-done((bf16[16,1,8,256]{3,2,0,1:T(8,128)(2,1)S(1)}, bf16[16,1,8,256]{3,2,0,1:T(8,128)(2,1)S(1)}, u32[]{:S(2)}, u32[]{:S(2)}) %collective-permute-start.4) | collective-permute-done | bytes 65568 | tf_op jit(solution)/shard_map/ppermute | solution.py:21
  66.9 173.5 %while.20 = (s32[]{:T(128)}, f32[12,8,512]{2,1,0:T(8,128)}, pred[12,32]{1,0:T(8,128)(4,1)S(1)}, s32[12,32]{1,0:T(8,128)S(1)}, bf16[36,8,128]{2,1,0:T(8,128)(2,1)...) while((s32[]{:T(128)}, f32[12,8,512]{2,1,0:T(8,128)}, ...), condition=%wide.region_7.8_spmd, body=%wide.region_4.7_spmd.sunk | while | flops 479064672 | bytes 19260240 | solution.py:99
  67.6 4.5 %fusion.89 = f32[512,32,128]{2,0,1:T(8,128)} fusion(bf16[32,64,128]{2,1,0:T(8,128)(2,1)S(1)} %gather_fusion, bf16[12,64,512]{2,1,0:T(8,128)(2,1)S(1)} %get-tuple-element.217, s32[]{:T(128)S(6)} %copy.50), kind=kOutput, calls=%fused_computation.19.clone.1 | convolution fusion | flops 268435456 | bytes 8978436 | tf_op jit(solution)/shard_map/while/body/eval_jaxpr/dr,mdc->rmc/dot_general | solution.py:36
  72.9 8.5 %fusion.90 = f32[12,8,512]{2,1,0:T(8,128)} fusion(f32[12,8,512]{2,1,0:T(8,128)} %get-tuple-element.205, s32[]{:T(128)S(6)} %copy.50, f32[512,32,128]{2,0,1:T(8,128)} %fusion.89, f32[32,128]{1,0:T(8,128)S(1)} %multiply_reduce_fusion.8, f32[512]{0:T(512)S(1)} %multiply_reduce_fusion.9, bf16[32,8,128]{2,1,0:T(8,128)(2,1)S(1)} %gather_fusion.1, ...), kind=kOutput, calls=%fused_computation.16.clone.1 | convolution fusion | flops 209747968 | bytes 8488996 | tf_op jit(solution)/shard_map/while/body/eval_jaxpr/rmc,mkc->kr/dot_general | solution.py:40
  87.4 8.5 %fusion.90 = f32[12,8,512]{2,1,0:T(8,128)} fusion(f32[12,8,512]{2,1,0:T(8,128)} %get-tuple-element.205, s32[]{:T(128)S(6)} %copy.50, f32[512,32,128]{2,0,1:T(8,128)} %fusion.89, f32[32,128]{1,0:T(8,128)S(1)} %multiply_reduce_fusion.8, f32[512]{0:T(512)S(1)} %multiply_reduce_fusion.9, bf16[32,8,128]{2,1,0:T(8,128)(2,1)S(1)} %gather_fusion.1, ...), kind=kOutput, calls=%fused_computation.16.clone.1 | convolution fusion | flops 209747968 | bytes 8488996 | tf_op jit(solution)/shard_map/while/body/eval_jaxpr/rmc,mkc->kr/dot_general | solution.py:40
  101.8 8.5 %fusion.90 = f32[12,8,512]{2,1,0:T(8,128)} fusion(f32[12,8,512]{2,1,0:T(8,128)} %get-tuple-element.205, s32[]{:T(128)S(6)} %copy.50, f32[512,32,128]{2,0,1:T(8,128)} %fusion.89, f32[32,128]{1,0:T(8,128)S(1)} %multiply_reduce_fusion.8, f32[512]{0:T(512)S(1)} %multiply_reduce_fusion.9, bf16[32,8,128]{2,1,0:T(8,128)(2,1)S(1)} %gather_fusion.1, ...), kind=kOutput, calls=%fused_computation.16.clone.1 | convolution fusion | flops 209747968 | bytes 8488996 | tf_op jit(solution)/shard_map/while/body/eval_jaxpr/rmc,mkc->kr/dot_general | solution.py:40
  111.0 4.5 %fusion.89 = f32[512,32,128]{2,0,1:T(8,128)} fusion(bf16[32,64,128]{2,1,0:T(8,128)(2,1)S(1)} %gather_fusion, bf16[12,64,512]{2,1,0:T(8,128)(2,1)S(1)} %get-tuple-element.217, s32[]{:T(128)S(6)} %copy.50), kind=kOutput, calls=%fused_computation.19.clone.1 | convolution fusion | flops 268435456 | bytes 8978436 | tf_op jit(solution)/shard_map/while/body/eval_jaxpr/dr,mdc->rmc/dot_general | solution.py:36
  116.3 8.5 %fusion.90 = f32[12,8,512]{2,1,0:T(8,128)} fusion(f32[12,8,512]{2,1,0:T(8,128)} %get-tuple-element.205, s32[]{:T(128)S(6)} %copy.50, f32[512,32,128]{2,0,1:T(8,128)} %fusion.89, f32[32,128]{1,0:T(8,128)S(1)} %multiply_reduce_fusion.8, f32[512]{0:T(512)S(1)} %multiply_reduce_fusion.9, bf16[32,8,128]{2,1,0:T(8,128)(2,1)S(1)} %gather_fusion.1, ...), kind=kOutput, calls=%fused_computation.16.clone.1 | convolution fusion | flops 209747968 | bytes 8488996 | tf_op jit(solution)/shard_map/while/body/eval_jaxpr/rmc,mkc->kr/dot_general | solution.py:40
  125.4 4.5 %fusion.89 = f32[512,32,128]{2,0,1:T(8,128)} fusion(bf16[32,64,128]{2,1,0:T(8,128)(2,1)S(1)} %gather_fusion, bf16[12,64,512]{2,1,0:T(8,128)(2,1)S(1)} %get-tuple-element.217, s32[]{:T(128)S(6)} %copy.50), kind=kOutput, calls=%fused_computation.19.clone.1 | convolution fusion | flops 268435456 | bytes 8978436 | tf_op jit(solution)/shard_map/while/body/eval_jaxpr/dr,mdc->rmc/dot_general | solution.py:36
  130.7 8.5 %fusion.90 = f32[12,8,512]{2,1,0:T(8,128)} fusion(f32[12,8,512]{2,1,0:T(8,128)} %get-tuple-element.205, s32[]{:T(128)S(6)} %copy.50, f32[512,32,128]{2,0,1:T(8,128)} %fusion.89, f32[32,128]{1,0:T(8,128)S(1)} %multiply_reduce_fusion.8, f32[512]{0:T(512)S(1)} %multiply_reduce_fusion.9, bf16[32,8,128]{2,1,0:T(8,128)(2,1)S(1)} %gather_fusion.1, ...), kind=kOutput, calls=%fused_computation.16.clone.1 | convolution fusion | flops 209747968 | bytes 8488996 | tf_op jit(solution)/shard_map/while/body/eval_jaxpr/rmc,mkc->kr/dot_general | solution.py:40
  139.9 4.5 %fusion.89 = f32[512,32,128]{2,0,1:T(8,128)} fusion(bf16[32,64,128]{2,1,0:T(8,128)(2,1)S(1)} %gather_fusion, bf16[12,64,512]{2,1,0:T(8,128)(2,1)S(1)} %get-tuple-element.217, s32[]{:T(128)S(6)} %copy.50), kind=kOutput, calls=%fused_computation.19.clone.1 | convolution fusion | flops 268435456 | bytes 8978436 | tf_op jit(solution)/shard_map/while/body/eval_jaxpr/dr,mdc->rmc/dot_general | solution.py:36
  145.2 8.5 %fusion.90 = f32[12,8,512]{2,1,0:T(8,128)} fusion(f32[12,8,512]{2,1,0:T(8,128)} %get-tuple-element.205, s32[]{:T(128)S(6)} %copy.50, f32[512,32,128]{2,0,1:T(8,128)} %fusion.89, f32[32,128]{1,0:T(8,128)S(1)} %multiply_reduce_fusion.8, f32[512]{0:T(512)S(1)} %multiply_reduce_fusion.9, bf16[32,8,128]{2,1,0:T(8,128)(2,1)S(1)} %gather_fusion.1, ...), kind=kOutput, calls=%fused_computation.16.clone.1 | convolution fusion | flops 209747968 | bytes 8488996 | tf_op jit(solution)/shard_map/while/body/eval_jaxpr/rmc,mkc->kr/dot_general | solution.py:40
  159.6 8.5 %fusion.90 = f32[12,8,512]{2,1,0:T(8,128)} fusion(f32[12,8,512]{2,1,0:T(8,128)} %get-tuple-element.205, s32[]{:T(128)S(6)} %copy.50, f32[512,32,128]{2,0,1:T(8,128)} %fusion.89, f32[32,128]{1,0:T(8,128)S(1)} %multiply_reduce_fusion.8, f32[512]{0:T(512)S(1)} %multiply_reduce_fusion.9, bf16[32,8,128]{2,1,0:T(8,128)(2,1)S(1)} %gather_fusion.1, ...), kind=kOutput, calls=%fused_computation.16.clone.1 | convolution fusion | flops 209747968 | bytes 8488996 | tf_op jit(solution)/shard_map/while/body/eval_jaxpr/rmc,mkc->kr/dot_general | solution.py:40
  174.1 8.5 %fusion.90 = f32[12,8,512]{2,1,0:T(8,128)} fusion(f32[12,8,512]{2,1,0:T(8,128)} %get-tuple-element.205, s32[]{:T(128)S(6)} %copy.50, f32[512,32,128]{2,0,1:T(8,128)} %fusion.89, f32[32,128]{1,0:T(8,128)S(1)} %multiply_reduce_fusion.8, f32[512]{0:T(512)S(1)} %multiply_reduce_fusion.9, bf16[32,8,128]{2,1,0:T(8,128)(2,1)S(1)} %gather_fusion.1, ...), kind=kOutput, calls=%fused_computation.16.clone.1 | convolution fusion | flops 209747968 | bytes 8488996 | tf_op jit(solution)/shard_map/while/body/eval_jaxpr/rmc,mkc->kr/dot_general | solution.py:40
  188.5 8.5 %fusion.90 = f32[12,8,512]{2,1,0:T(8,128)} fusion(f32[12,8,512]{2,1,0:T(8,128)} %get-tuple-element.205, s32[]{:T(128)S(6)} %copy.50, f32[512,32,128]{2,0,1:T(8,128)} %fusion.89, f32[32,128]{1,0:T(8,128)S(1)} %multiply_reduce_fusion.8, f32[512]{0:T(512)S(1)} %multiply_reduce_fusion.9, bf16[32,8,128]{2,1,0:T(8,128)(2,1)S(1)} %gather_fusion.1, ...), kind=kOutput, calls=%fused_computation.16.clone.1 | convolution fusion | flops 209747968 | bytes 8488996 | tf_op jit(solution)/shard_map/while/body/eval_jaxpr/rmc,mkc->kr/dot_general | solution.py:40
  197.7 4.5 %fusion.89 = f32[512,32,128]{2,0,1:T(8,128)} fusion(bf16[32,64,128]{2,1,0:T(8,128)(2,1)S(1)} %gather_fusion, bf16[12,64,512]{2,1,0:T(8,128)(2,1)S(1)} %get-tuple-element.217, s32[]{:T(128)S(6)} %copy.50), kind=kOutput, calls=%fused_computation.19.clone.1 | convolution fusion | flops 268435456 | bytes 8978436 | tf_op jit(solution)/shard_map/while/body/eval_jaxpr/dr,mdc->rmc/dot_general | solution.py:36
  203.0 8.5 %fusion.90 = f32[12,8,512]{2,1,0:T(8,128)} fusion(f32[12,8,512]{2,1,0:T(8,128)} %get-tuple-element.205, s32[]{:T(128)S(6)} %copy.50, f32[512,32,128]{2,0,1:T(8,128)} %fusion.89, f32[32,128]{1,0:T(8,128)S(1)} %multiply_reduce_fusion.8, f32[512]{0:T(512)S(1)} %multiply_reduce_fusion.9, bf16[32,8,128]{2,1,0:T(8,128)(2,1)S(1)} %gather_fusion.1, ...), kind=kOutput, calls=%fused_computation.16.clone.1 | convolution fusion | flops 209747968 | bytes 8488996 | tf_op jit(solution)/shard_map/while/body/eval_jaxpr/rmc,mkc->kr/dot_general | solution.py:40
  212.1 4.5 %fusion.89 = f32[512,32,128]{2,0,1:T(8,128)} fusion(bf16[32,64,128]{2,1,0:T(8,128)(2,1)S(1)} %gather_fusion, bf16[12,64,512]{2,1,0:T(8,128)(2,1)S(1)} %get-tuple-element.217, s32[]{:T(128)S(6)} %copy.50), kind=kOutput, calls=%fused_computation.19.clone.1 | convolution fusion | flops 268435456 | bytes 8978436 | tf_op jit(solution)/shard_map/while/body/eval_jaxpr/dr,mdc->rmc/dot_general | solution.py:36
  217.4 8.5 %fusion.90 = f32[12,8,512]{2,1,0:T(8,128)} fusion(f32[12,8,512]{2,1,0:T(8,128)} %get-tuple-element.205, s32[]{:T(128)S(6)} %copy.50, f32[512,32,128]{2,0,1:T(8,128)} %fusion.89, f32[32,128]{1,0:T(8,128)S(1)} %multiply_reduce_fusion.8, f32[512]{0:T(512)S(1)} %multiply_reduce_fusion.9, bf16[32,8,128]{2,1,0:T(8,128)(2,1)S(1)} %gather_fusion.1, ...), kind=kOutput, calls=%fused_computation.16.clone.1 | convolution fusion | flops 209747968 | bytes 8488996 | tf_op jit(solution)/shard_map/while/body/eval_jaxpr/rmc,mkc->kr/dot_general | solution.py:40
  231.9 8.5 %fusion.90 = f32[12,8,512]{2,1,0:T(8,128)} fusion(f32[12,8,512]{2,1,0:T(8,128)} %get-tuple-element.205, s32[]{:T(128)S(6)} %copy.50, f32[512,32,128]{2,0,1:T(8,128)} %fusion.89, f32[32,128]{1,0:T(8,128)S(1)} %multiply_reduce_fusion.8, f32[512]{0:T(512)S(1)} %multiply_reduce_fusion.9, bf16[32,8,128]{2,1,0:T(8,128)(2,1)S(1)} %gather_fusion.1, ...), kind=kOutput, calls=%fused_computation.16.clone.1 | convolution fusion | flops 209747968 | bytes 8488996 | tf_op jit(solution)/shard_map/while/body/eval_jaxpr/rmc,mkc->kr/dot_general | solution.py:40
  240.4 84.0 %while.21 = (s32[]{:T(128)}, f32[12,8,128]{2,1,0:T(8,128)S(1)}, s32[12,32]{1,0:T(8,128)}, bf16[32,8,256]{2,1,0:T(8,128)(2,1)S(1)}, bf16[12,64,128]{2,1,0:T(8,128...) while((s32[]{:T(128)}, f32[12,8,128]{2,1,0:T(8,128)S(1)}, s32[12,32]{1,0:T(8,128)}, ...), condition=%wide.region_12.13_spmd, body=%wide.region_9.12_spmd.sunk | while | flops 240665568 | bytes 13084389 | solution.py:114
  (252 shorter events, 158.0 us)
Async XLA Ops:
  7.4 59.5 %copy-start = (bf16[12,64,128]{2,1,0:T(8,128)(2,1)S(1)}, bf16[12,64,128]{2,1,0:T(8,128)(2,1)}, u32[]{:S(2)}) copy-start(bf16[12,64,128]{2,1,0:T(8,128)(2,1)} %param.10) | copy-start | bytes 589828
  7.4 49.6 %copy-start.1 = (bf16[12,8,128]{2,1,0:T(8,128)(2,1)S(1)}, bf16[12,8,128]{2,1,0:T(8,128)(2,1)}, u32[]{:S(2)}) copy-start(bf16[12,8,128]{2,1,0:T(8,128)(2,1)} %param.11) | copy-start | bytes 73732
  9.1 22.0 %all-to-all-start = ((s32[8,1,12]{2,1,0:T(1,128)}), s32[8,1,12]{2,1,0:T(1,128)S(1)}, u32[]{:S(2)}, u32[]{:S(2)}) async-start(s32[8,1,12]{2,1,0:T(1,128)} %bitcast.13), calls=%async_computation | async-start | bytes 8192 | tf_op jit(solution)/shard_map/all_to_all | solution.py:60
  16.3 224.1 %all-gather.2.cloned.1.call-start = ((), (), s32[]{:S(2)}) async-start(), calls=%async_computation.5 | async-start | bytes 1081344 | tf_op jit(solution)/shard_map/all_gather | solution.py:106
  16.4 14.9 %collective-permute-start = (bf16[1,1,8,256]{3,2,1,0:T(8,128)(2,1)}, bf16[1,1,8,256]{3,2,1,0:T(8,128)(2,1)S(1)}, u32[]{:S(2)}, u32[]{:S(2)}) collective-permute-start(bf16[1,1,8,256]{3,2,1,0:T(8,128)(2,1)} %bitcast.136), channel_id=1, source_target_pairs={{0,1},{1,0},{2,3},{3,2},{4,5},{5,4},{6,7},{7,6},{8,9},{9,8},{10,11... | collective-permute-start | bytes 12296 | tf_op jit(solution)/shard_map/ppermute | solution.py:21
  32.0 3.7 %collective-permute-start.1 = (bf16[2,1,8,256]{3,2,0,1:T(8,128)(2,1)S(1)}, bf16[2,1,8,256]{3,2,0,1:T(8,128)(2,1)S(1)}, u32[]{:S(2)}, u32[]{:S(2)}) collective-permute-start(bf16[2,1,8,256]{3,2,0,1:T(8,128)(2,1)S(1)} %get-tuple-element.115), channel_id=1, source_target_pairs={{0,2},{1,3},{2,0},{3,1},{4,6},{5,7},{6,4},{7,5},{8,10},{9,11},{10,... | collective-permute-start | bytes 24584 | tf_op jit(solution)/shard_map/ppermute | solution.py:21
  35.7 8.0 %collective-permute-start.2 = (bf16[4,1,8,256]{3,2,0,1:T(8,128)(2,1)S(1)}, bf16[4,1,8,256]{3,2,0,1:T(8,128)(2,1)S(1)}, u32[]{:S(2)}, u32[]{:S(2)}) collective-permute-start(bf16[4,1,8,256]{3,2,0,1:T(8,128)(2,1)S(1)} %bitcast.127), channel_id=1, source_target_pairs={{0,4},{1,5},{2,6},{3,7},{4,0},{5,1},{6,2},{7,3},{8,12},{9,13},{10,... | collective-permute-start | bytes 49160 | tf_op jit(solution)/shard_map/ppermute | solution.py:21
  39.2 11.4 %all-to-all-start.1 = ((bf16[8,3,8,128]{3,2,1,0:T(8,128)(2,1)}), bf16[8,3,8,128]{3,2,1,0:T(8,128)(2,1)S(1)}, u32[]{:S(2)}, u32[]{:S(2)}) async-start(bf16[8,3,8,128]{3,2,1,0:T(8,128)(2,1)} %copy.31), calls=%async_computation.1 | async-start | bytes 98304 | tf_op jit(solution)/shard_map/all_to_all | solution.py:74
  43.7 10.3 %collective-permute-start.3 = (bf16[8,1,8,256]{3,2,0,1:T(8,128)(2,1)S(1)}, bf16[8,1,8,256]{3,2,0,1:T(8,128)(2,1)S(1)}, u32[]{:S(2)}, u32[]{:S(2)}) collective-permute-start(bf16[8,1,8,256]{3,2,0,1:T(8,128)(2,1)S(1)} %bitcast.125), channel_id=1, source_target_pairs={{0,8},{1,9},{2,10},{3,11},{4,12},{5,13},{6,14},{7,15},{8,0},{9,1},... | collective-permute-start | bytes 98312 | tf_op jit(solution)/shard_map/ppermute | solution.py:21
  50.5 16.3 %all-to-all-start.2 = ((bf16[8,3,64,128]{3,2,1,0:T(8,128)(2,1)}), bf16[8,3,64,128]{3,2,1,0:T(8,128)(2,1)S(1)}, u32[]{:S(2)}, u32[]{:S(2)}) async-start(bf16[8,3,64,128]{3,2,1,0:T(8,128)(2,1)} %copy.33), calls=%async_computation.2 | async-start | bytes 786432 | tf_op jit(solution)/shard_map/all_to_all | solution.py:73
  54.0 270.4 %reduce-scatter.2.cloned.1.call-start = ((), (), s32[]{:S(2)}) async-start(), calls=%async_computation.4 | async-start | bytes 245760 | tf_op jit(solution)/shard_map/reduce_scatter | solution.py:100
  54.1 12.7 %collective-permute-start.4 = (bf16[16,1,8,256]{3,2,0,1:T(8,128)(2,1)S(1)}, bf16[16,1,8,256]{3,2,0,1:T(8,128)(2,1)S(1)}, u32[]{:S(2)}, u32[]{:S(2)}) collective-permute-start(bf16[16,1,8,256]{3,2,0,1:T(8,128)(2,1)S(1)} %bitcast.122), channel_id=1, source_target_pairs={{0,16},{1,17},{2,18},{3,19},{4,20},{5,21},{6,22},{7,23},{8,24},{9,... | collective-permute-start | bytes 196616 | tf_op jit(solution)/shard_map/ppermute | solution.py:21
Sparse Core Ops, SparseCore 0:
  20.8 57.6 all-gather.1
Sparse Core Ops, SparseCore 1:
  240.5 19.1 reduce-scatter.1
